TPU v7x, 512 devices: a whole 4x4x16 slice. The times are simulated.
512 devices in a mesh: dp: 64 (over y, z_hi, x, core), fsdp: 8 (over z_lo).
Axes of the slice: x: 4, y: 4, z: 16 (z_hi: 2, z_lo: 8; z = z_hi * 8 + z_lo), core: 2. Of those that a mesh axis runs over, the one named last changes fastest.
Arguments:
- inputs: bfloat16 [65536, 4096], P(('dp', 'fsdp')), may hold values from -6 to 6
- out_grad: bfloat16 [65536, 2048], P(('dp', 'fsdp')), may hold values from -24 to 24
- weight: bfloat16 [4096, 2048], P('fsdp'), may hold values from -0.125 to 0.125
- proj_basis: bfloat16 [4096, 256], P('fsdp'), may hold values from -0.09375 to 0.09375
- first_moment: float32 [64, 8192], P('dp'), may hold values from -6 to 6
- second_moment: float32 [64, 8192], P('dp'), may hold values from 0.25 to 4
Outputs:
- input_grad: bfloat16 [65536, 4096], P(('dp', 'fsdp'))
- new_first: float32 [64, 8192], P('dp')
- new_second: float32 [64, 8192], P('dp')
- update: float32 [4096, 2048], P('fsdp', 'dp')
All inputs are finite; a program needn't handle non-finite values.
Results may differ from a plain program's by a relative error of at most 0.0029.
Values may be sent and summed in bfloat16 or wider, within the bound.
No kernel may reach another device: no remote copies, remote signals or barrier semaphores. Data moves between devices by JAX's collectives and lax.ppermute only.
A program may use at most 64 MiB of HBM per device.

v0:
```python
import math
import jax
import jax.numpy as jnp
from jax import lax
from jax.sharding import PartitionSpec as P

STEP = 1000
beta_one = 0.9
beta_two = 0.999
epsilon = 1e-08


def on_device(inputs, out_grad, weight, proj_basis, first_moment, second_moment):
    tok_rows = inputs.shape[0]
    data_count = lax.axis_size("dp")
    shard_count = lax.axis_size("fsdp")
    rank_cols = proj_basis.shape[1]
    feature_grad = lax.dot_general(
        lax.all_gather(out_grad, "fsdp", axis=0, tiled=True),
        weight,
        (((1,), (1,)), ((), ())),
        preferred_element_type=jnp.float32,
    ).astype(jnp.bfloat16)
    input_grad = lax.all_to_all(feature_grad, "fsdp", split_axis=0, concat_axis=1, tiled=True)
    proj_full = jnp.dot(
        inputs,
        lax.all_gather(proj_basis, "fsdp", axis=0, tiled=True),
        preferred_element_type=jnp.float32,
    )
    projected_in = proj_full.astype(jnp.bfloat16)
    scale_factor = 1.0 / math.sqrt(tok_rows * data_count * shard_count)
    low_rank = (
        lax.dot_general(
            projected_in, out_grad, (((0,), (0,)), ((), ())), preferred_element_type=jnp.float32
        )
        * scale_factor
    )
    col_width = low_rank.shape[1] // data_count
    summed = lax.psum(low_rank, ("dp", "fsdp"))
    grad_block = lax.dynamic_slice_in_dim(summed, lax.axis_index("dp") * col_width, col_width, 1)
    flat_grad = grad_block.reshape(1, rank_cols * col_width)
    new_first = beta_one * first_moment + (1.0 - beta_one) * flat_grad
    new_second = beta_two * second_moment + (1.0 - beta_two) * flat_grad * flat_grad
    corr_one = 1.0 - beta_one**STEP
    corr_two = 1.0 - beta_two**STEP
    direction = (new_first / corr_one / (jnp.sqrt(new_second / corr_two) + epsilon)).astype(
        jnp.bfloat16
    )
    direction = direction.reshape(rank_cols, col_width)
    update = jnp.dot(proj_basis, direction, preferred_element_type=jnp.float32)
    return (input_grad, new_first, new_second, update)


def solution(mesh):
    in_specs = (
        P(("dp", "fsdp"), None),
        P(("dp", "fsdp"), None),
        P("fsdp", None),
        P("fsdp", None),
        P("dp", None),
        P("dp", None),
    )
    out_specs = (P(("dp", "fsdp"), None), P("dp", None), P("dp", None), P("fsdp", "dp"))
    return jax.shard_map(
        on_device, mesh=mesh, in_specs=in_specs, out_specs=out_specs, check_vma=False
    )
```

profile of v0, /device:TPU:1, one launch (start us, length us, event | category | flops | bytes accessed | tf_op | source)
XLA Modules:
  0.0 714.3 jit_solution(5845049301039747095)
XLA Ops:
  7.2 0.0 copy-start
  7.2 0.0 all-gather.3.cloned.1.call-start
  7.2 0.7 all-gather.3.cloned.1.call-update
  7.9 0.0 all-gather.5.cloned.1.call-start
  8.0 0.7 all-gather.5.cloned.1.call-update
  8.7 111.0 %all-gather.3.cloned.1.call-done = bf16[1024,2048]{1,0:T(8,128)(2,1)} async-done(((bf16[128,2048]{1,0:T(8,128)(2,1)}), bf16[1024,2048]{1,0:T(8,128)(2,1)}) %all-gather.3.cloned.1.call-update) | async-done | bytes 4194320 | tf_op jit(solution)/shard_map/all_gather | solution.py:19
  119.7 0.0 copy-done
  119.7 5.5 convolution_convert_fusion
  125.2 3.6 all-to-all-start
  128.8 0.0 all-reduce.2.cloned.1.call-start
  128.8 89.4 %all-gather.5.cloned.1.call-done = bf16[4096,256]{1,0:T(8,128)(2,1)} async-done(((bf16[512,256]{1,0:T(8,128)(2,1)}), bf16[4096,256]{1,0:T(8,128)(2,1)}) %all-gather.5.cloned.1.call-update) | async-done | bytes 2097168 | tf_op jit(solution)/shard_map/all_gather | solution.py:27
  218.2 4.7 convolution_multiply_fusion
  222.9 0.0 copy-start.1
  222.9 0.0 all-reduce.2.cloned.1.call-update
  222.9 478.2 %all-reduce.2.cloned.1.call-done = f32[256,2048]{0,1:T(8,128)} async-done(((f32[256,2048]{0,1:T(8,128)}), f32[256,2048]{0,1:T(8,128)}) %all-reduce.2.cloned.1.call-update) | async-done | bytes 2097168 | tf_op jit(solution)/shard_map/psum | solution.py:39
  701.2 1.4 constant_dynamic-slice_fusion
  702.5 0.9 copy.12
  703.4 0.7 reshape.53
  704.1 1.6 convert_reduce_fusion
  705.7 0.1 reshape.54
  705.8 0.0 copy-done.1
  705.8 0.8 convolution_bitcast_fusion
  706.7 0.0 all-to-all-done
  706.7 1.1 copy.13
Async XLA Ops:
  7.2 112.5 %copy-start = (bf16[512,2048]{1,0:T(8,128)(2,1)S(1)}, bf16[512,2048]{1,0:T(8,128)(2,1)}, u32[]{:S(2)}) copy-start(bf16[512,2048]{1,0:T(8,128)(2,1)} %param.8) | copy-start | bytes 6291460
  7.2 112.5 %all-gather.3.cloned.1.call-start = ((), (), s32[]{:S(2)}) async-start(), calls=%async_computation.1 | async-start | bytes 4718592 | tf_op jit(solution)/shard_map/all_gather | solution.py:19
  7.9 210.3 %all-gather.5.cloned.1.call-start = ((), (), s32[]{:S(2)}) async-start(), calls=%async_computation.2 | async-start | bytes 2359296 | tf_op jit(solution)/shard_map/all_gather | solution.py:27
  125.2 581.5 %all-to-all-start = ((bf16[8,128,512]{2,1,0:T(8,128)(2,1)}), bf16[8,128,512]{2,1,0:T(8,128)(2,1)S(1)}, u32[]{:S(2)}, u32[]{:S(2)}) async-start(bf16[8,128,512]{2,1,0:T(8,128)(2,1)} %bitcast.14), calls=%async_computation | async-start | bytes 2097152 | tf_op jit(solution)/shard_map/all_to_all | solution.py:24
  128.8 572.4 %all-reduce.2.cloned.1.call-start = ((), (), s32[]{:S(2)}) async-start(), calls=%async_computation.3 | async-start | bytes 4194304 | tf_op jit(solution)/shard_map/psum | solution.py:39
  222.9 482.9 %copy-start.1 = (bf16[512,256]{1,0:T(8,128)(2,1)S(1)}, bf16[512,256]{1,0:T(8,128)(2,1)}, u32[]{:S(2)}) copy-start(bf16[512,256]{1,0:T(8,128)(2,1)} %param.9) | copy-start | bytes 786436
Sparse Core Ops, SparseCore 0:
  10.1 109.5 all-gather.2
  121.8 96.4 all-gather.4
  223.6 477.5 all-reduce.1
where the time goes:
time: 715 us; the launch traced here: 714 us
  waiting for transfers between devices  680 us (95%)
  between operations  13.8 us (2%)
  matrix products  11 us (2%)
    psum x1, waiting for transfers between devices, on_device(): summed = lax.psum(low_rank, ('dp', 'fsdp'))  478 us
    all_gather x1, waiting for transfers between devices, on_device(): lax.all_gather(out_grad, 'fsdp', axis=0, tiled=True)  111 us
    all_gather x1, waiting for transfers between devices, on_device(): lax.all_gather(proj_basis, 'fsdp', axis=0, tiled=True)  89.4 us
  transfers between devices with their start and end apart: 4, of which 3 were waited for; matrix products, arithmetic and copies ran while one was open for 2% of the time, Pallas kernels for 0%

commit v1 on v0

--- a/solution.py
+++ b/solution.py
@@ -36,7 +36,7 @@
         * scale_factor
     )
     col_width = low_rank.shape[1] // data_count
-    summed = lax.psum(low_rank, ("dp", "fsdp"))
+    summed = lax.psum(lax.psum(low_rank, "fsdp"), "dp")
     grad_block = lax.dynamic_slice_in_dim(summed, lax.axis_index("dp") * col_width, col_width, 1)
     flat_grad = grad_block.reshape(1, rank_cols * col_width)
     new_first = beta_one * first_moment + (1.0 - beta_one) * flat_grad

time: 715 us -> 1450 us (2.03)
  waiting for transfers between devices: 680 us -> 1420 us
    psum x1 -> x2, waiting for transfers between devices: 478 us -> 1240 us  [on_device(): summed = lax.psum(lax.psum(low_rank, 'fsdp'), 'dp')]
    all_gather x1, waiting for transfers between devices: 89.4 us -> 72.6 us  [on_device(): lax.all_gather(proj_basis, 'fsdp', axis=0, tiled=True)]
  transfers between devices with their start and end apart: 4 -> 5, of which waited for: 3 -> 4; matrix products, arithmetic and copies ran while one was open for 2% -> 1% of each run, Pallas kernels for 0% -> 0%
where the time goes in v1:
time: 1450 us
  waiting for transfers between devices  1420 us (98%)
    psum x2, waiting for transfers between devices, on_device(): summed = lax.psum(lax.psum(low_rank, 'fsdp'), 'dp')  1240 us
    all_gather x1, waiting for transfers between devices, on_device(): lax.all_gather(out_grad, 'fsdp', axis=0, tiled=True)  103 us
    all_gather x1, waiting for transfers between devices, on_device(): lax.all_gather(proj_basis, 'fsdp', axis=0, tiled=True)  72.6 us
  transfers between devices with their start and end apart: 5, of which 4 were waited for; matrix products, arithmetic and copies ran while one was open for 1% of the time, Pallas kernels for 0%

profile of v1, /device:TPU:1, one launch (start us, length us, event | category | flops | bytes accessed | tf_op | source)
XLA Modules:
  0.0 1453.4 jit_solution(15406085166230876925)
XLA Ops:
  7.2 0.0 copy-start
  7.2 0.0 all-gather.5.cloned.1.call-start
  7.2 0.7 all-gather.5.cloned.1.call-update
  7.9 0.0 all-gather.3.cloned.1.call-start
  8.0 0.7 all-gather.3.cloned.1.call-update
  8.7 0.0 all-reduce.3.cloned.1.call-start
  8.7 72.6 %all-gather.5.cloned.1.call-done = bf16[4096,256]{1,0:T(8,128)(2,1)} async-done(((bf16[512,256]{1,0:T(8,128)(2,1)}), bf16[4096,256]{1,0:T(8,128)(2,1)}) %all-gather.5.cloned.1.call-update) | async-done | bytes 2097168 | tf_op jit(solution)/shard_map/all_gather | solution.py:27
  81.3 4.7 convolution_multiply_fusion
  86.0 0.0 all-reduce.3.cloned.1.call-update
  86.0 102.5 %all-gather.3.cloned.1.call-done = bf16[1024,2048]{1,0:T(8,128)(2,1)} async-done(((bf16[128,2048]{1,0:T(8,128)(2,1)}), bf16[1024,2048]{1,0:T(8,128)(2,1)}) %all-gather.3.cloned.1.call-update) | async-done | bytes 4194320 | tf_op jit(solution)/shard_map/all_gather | solution.py:19
  188.5 0.0 copy-done
  188.5 5.5 convolution_convert_fusion
  194.0 0.0 copy-start.1
  194.0 3.7 all-to-all-start
  197.7 0.0 all-reduce.5.cloned.1.call-start
  197.8 157.3 %all-reduce.3.cloned.1.call-done = f32[256,2048]{0,1:T(8,128)} async-done(((f32[256,2048]{0,1:T(8,128)}), f32[256,2048]{0,1:T(8,128)}) %all-reduce.3.cloned.1.call-update) | async-done | bytes 2097168 | tf_op jit(solution)/shard_map/psum | solution.py:39
  355.1 0.0 all-reduce.5.cloned.1.call-update
  355.1 1085.2 %all-reduce.5.cloned.1.call-done = f32[256,2048]{0,1:T(8,128)} async-done(((f32[256,2048]{0,1:T(8,128)}), f32[256,2048]{0,1:T(8,128)}) %all-reduce.5.cloned.1.call-update) | async-done | bytes 2097168 | tf_op jit(solution)/shard_map/psum | solution.py:39
  1440.3 1.4 constant_dynamic-slice_fusion
  1441.7 0.9 copy.12
  1442.6 0.7 reshape.53
  1443.3 1.6 convert_reduce_fusion
  1444.9 0.1 reshape.54
  1445.0 0.0 copy-done.1
  1445.0 0.8 convolution_bitcast_fusion
  1445.8 0.0 all-to-all-done
  1445.8 1.1 copy.13
Async XLA Ops:
  7.2 181.3 %copy-start = (bf16[512,2048]{1,0:T(8,128)(2,1)S(1)}, bf16[512,2048]{1,0:T(8,128)(2,1)}, u32[]{:S(2)}) copy-start(bf16[512,2048]{1,0:T(8,128)(2,1)} %param.8) | copy-start | bytes 6291460
  7.2 74.1 %all-gather.5.cloned.1.call-start = ((), (), s32[]{:S(2)}) async-start(), calls=%async_computation.2 | async-start | bytes 2359296 | tf_op jit(solution)/shard_map/all_gather | solution.py:27
  7.9 180.6 %all-gather.3.cloned.1.call-start = ((), (), s32[]{:S(2)}) async-start(), calls=%async_computation.1 | async-start | bytes 4718592 | tf_op jit(solution)/shard_map/all_gather | solution.py:19
  8.7 346.4 %all-reduce.3.cloned.1.call-start = ((), (), s32[]{:S(2)}) async-start(), calls=%async_computation.3 | async-start | bytes 4194304 | tf_op jit(solution)/shard_map/psum | solution.py:39
  194.0 1251.0 %copy-start.1 = (bf16[512,256]{1,0:T(8,128)(2,1)S(1)}, bf16[512,256]{1,0:T(8,128)(2,1)}, u32[]{:S(2)}) copy-start(bf16[512,256]{1,0:T(8,128)(2,1)} %param.9) | copy-start | bytes 786436
  194.0 1251.8 %all-to-all-start = ((bf16[8,128,512]{2,1,0:T(8,128)(2,1)}), bf16[8,128,512]{2,1,0:T(8,128)(2,1)S(1)}, u32[]{:S(2)}, u32[]{:S(2)}) async-start(bf16[8,128,512]{2,1,0:T(8,128)(2,1)} %bitcast.14), calls=%async_computation | async-start | bytes 2097152 | tf_op jit(solution)/shard_map/all_to_all | solution.py:24
  197.7 1242.6 %all-reduce.5.cloned.1.call-start = ((), (), s32[]{:S(2)}) async-start(), calls=%async_computation.4 | async-start | bytes 4194304 | tf_op jit(solution)/shard_map/psum | solution.py:39
Sparse Core Ops, SparseCore 0:
  10.1 71.1 all-gather.4
  83.3 105.0 all-gather.2
  191.4 163.6 all-reduce.2
  357.9 1082.4 all-reduce.4
